TPU v7x, 32 devices: a whole 2x2x4 slice. The times are simulated.
32 devices in a mesh: row: 4 (over z), col: 8 (over y, x, core).
Axes of the slice: x: 2, y: 2, z: 4, core: 2. Of those that a mesh axis runs over, the one named last changes fastest.
Arguments:
- slip_load: bfloat16 [4, 8, 1024, 128], P('row', 'col'), may hold values from -6 to 6
- flexibility: bfloat16 [4, 8, 1024, 1024], P('row', 'col'), as said below
- schur: bfloat16 [4, 8, 1024, 1024], P('row', 'col'), as said below
- corner_coupling: float32 [4, 8, 12, 1024], P('row', 'col'), may hold values from -0.1875 to 0.1875
- coarse_inverse: float32 [384, 384], P('row', 'col'), as said below
- bounds_table: float32 [16], replicated, may hold values from 0.3 to 3
- bound_index: int32 [4, 8, 1024], P('row', 'col'), may hold values from 0 to 15
- face_rows: int32 [4, 8, 4], P('row', 'col'), may hold values from 0 to 256, as said below
Outputs:
- multipliers: bfloat16 [4, 8, 1024, 128], P('row', 'col')
Inputs may be any that keep to these rules, and one draw needn't show every extreme that they name: `face_rows`: face counts agree between the two subdomains of a shared face, are 0 on faces at the edge of the grid, and some face has exactly 256 live slots. `coarse_inverse`: symmetric. `flexibility`: symmetric and positive definite. `schur`: symmetric and positive definite.
All inputs are finite; a program needn't handle non-finite values.
Results may differ from a plain program's by a relative error of at most 0.0038.
Values sent between devices are 32-bit elements; how exact they have to be, the bound alone decides.
No kernel may reach another device: no remote copies, remote signals or barrier semaphores. Data moves between devices by JAX's collectives and lax.ppermute only.
A program may use at most 64 MiB of HBM per device.

v0:
```python
import jax
import jax.numpy as jnp
from jax import lax
from jax.sharding import PartitionSpec as P

ITERS = 2


def passed_along(x, axis, by):
    count = lax.axis_size(axis)
    pairs = [(i, i + by) for i in range(count) if 0 <= i + by < count]
    return lax.ppermute(x, axis, pairs)


def broadcast(block, axis, holder):
    block = jnp.where(lax.axis_index(axis) == holder, block, jnp.zeros_like(block))
    return lax.psum(block, axis)


def local(
    slip_load,
    flexibility,
    schur,
    corner_coupling,
    coarse_inverse,
    bounds_table,
    bound_index,
    face_rows,
):
    loads = slip_load[0, 0].astype(jnp.float32)
    flex_block = flexibility[0, 0]
    schur_block = schur[0, 0]
    coupling = corner_coupling[0, 0]
    row_count = flex_block.shape[0]
    face_size = row_count // 4
    corners = coupling.shape[0]
    row_devices = lax.axis_size("row")
    row_index = lax.axis_index("row")
    col_index = lax.axis_index("col")
    levels = jnp.arange(bounds_table.shape[0], dtype=jnp.int32)
    onehot = (bound_index[0, 0][:, None] == levels[None, :]).astype(jnp.float32)
    bound = jnp.sum(onehot * bounds_table[None, :], axis=1)[:, None]
    slots = jnp.arange(face_size, dtype=jnp.int32)
    live = (slots[None, :] < face_rows[0, 0][:, None]).astype(jnp.float32).reshape(row_count, 1)
    lam = jnp.clip(loads, -bound, bound)
    for iteration in range(ITERS):
        displacement = jnp.dot(
            flex_block, lam.astype(jnp.bfloat16), preferred_element_type=jnp.float32
        )
        nb_west = passed_along(displacement[face_size : 2 * face_size], "col", 1)
        nb_east = passed_along(displacement[0:face_size], "col", -1)
        nb_lower = passed_along(displacement[3 * face_size :], "row", 1)
        nb_upper = passed_along(displacement[2 * face_size : 3 * face_size], "row", -1)
        paired = jnp.concatenate([nb_west, nb_east, nb_lower, nb_upper], axis=0)
        jump = live * (displacement - paired - loads)
        corner_force = jnp.dot(coupling, jump, precision=lax.Precision.HIGHEST)
        gathered = lax.all_gather(corner_force, "row", axis=0, tiled=True)
        partial_value = jnp.dot(coarse_inverse, gathered, precision=lax.Precision.HIGHEST)
        total = lax.psum(partial_value, "col")
        picked = broadcast(total, "row", col_index // 2)
        offset = col_index % 2 * (corners * row_devices) + row_index * corners
        coarse = lax.dynamic_slice_in_dim(picked, offset, corners, 0)
        correction = lax.dot_general(
            coupling, coarse, (((0,), (0,)), ((), ())), precision=lax.Precision.HIGHEST
        )
        projected = jump - correction
        projected_b = projected.astype(jnp.bfloat16)
        search = jnp.dot(schur_block, projected_b, preferred_element_type=jnp.float32)
        gain_local = jnp.sum(projected_b.astype(jnp.float32) * search, axis=0)
        search_b = search.astype(jnp.bfloat16)
        gain = lax.psum(gain_local, ("row", "col"))
        curved = jnp.dot(flex_block, search_b, preferred_element_type=jnp.float32)
        curvature = lax.psum(jnp.sum(search_b.astype(jnp.float32) * curved, axis=0), ("row", "col"))
        lam = jnp.clip(lam - (gain / curvature)[None, :] * search, -bound, bound)
    return lam.astype(jnp.bfloat16)[None, None]


def solution(mesh):
    return jax.shard_map(
        local,
        mesh=mesh,
        in_specs=(
            P("row", "col", None, None),
            P("row", "col", None, None),
            P("row", "col", None, None),
            P("row", "col", None, None),
            P("row", "col"),
            P(),
            P("row", "col", None),
            P("row", "col", None),
        ),
        out_specs=P("row", "col", None, None),
        check_vma=False,
    )
```

profile of v0, /device:TPU:14, one launch (start us, length us, event | category | flops | bytes accessed | tf_op | source)
XLA Modules:
  0.0 235.4 jit_solution(16768184671712670383)
XLA Ops:
  0.0 0.9 select_reduce_fusion
  1.0 1.1 copy.15
  2.1 2.4 %fusion.14 = f32[1024,128]{0,1:T(8,128)S(1)} fusion(bf16[1,1,1024,1024]{3,2,1,0:T(8,128)(2,1)} %param.9, bf16[1,1,1024,128]{2,3,1,0:T(8,128)(2,1)S(1)} %copy.15, f32[1024]{0:T(1024)S(1)} %neg.10, f32[1024]{0:T(1024)S(1)} %select_reduce_fusion), kind=kOutput, calls=%fused_computation.16 | convolution fusion | flops 269221888 | bytes 2891776 | tf_op jit(solution)/shard_map/dot_general | solution.py:47
  5.3 1.9 collective-permute-start
  7.2 2.4 %collective-permute-start.3 = (f32[256,128]{0,1:T(8,128)}, f32[256,128]{0,1:T(8,128)S(1)}, u32[]{:S(2)}, u32[]{:S(2)}) collective-permute-start(f32[256,128]{0,1:T(8,128)} %get-tuple-element.14), channel_id=1, source_target_pairs={{8,0},{16,8},{24,16},{9,1},{17,9},{25,17},{10,2},{18,10},{26,18},{... | collective-permute-start | bytes 393224 | tf_op jit(solution)/shard_map/ppermute | solution.py:12
  9.6 3.5 %collective-permute-start.2 = (f32[256,128]{0,1:T(8,128)}, f32[256,128]{0,1:T(8,128)S(1)}, u32[]{:S(2)}, u32[]{:S(2)}) collective-permute-start(f32[256,128]{0,1:T(8,128)} %get-tuple-element.15), channel_id=1, source_target_pairs={{0,8},{8,16},{16,24},{1,9},{9,17},{17,25},{2,10},{10,18},{18,26},{... | collective-permute-start | bytes 393224 | tf_op jit(solution)/shard_map/ppermute | solution.py:12
  13.1 3.1 %collective-permute-start.1 = (f32[256,128]{0,1:T(8,128)S(1)}, f32[256,128]{0,1:T(8,128)}, u32[]{:S(2)}, u32[]{:S(2)}) collective-permute-start(f32[256,128]{0,1:T(8,128)S(1)} %get-tuple-element.16), channel_id=1, source_target_pairs={{1,0},{2,1},{3,2},{4,3},{5,4},{6,5},{7,6},{9,8},{10,9},{11,10},{12... | collective-permute-start | bytes 393224 | tf_op jit(solution)/shard_map/ppermute | solution.py:12
  16.6 2.0 collective-permute-done.1
  18.7 1.5 convolution_bitcast_fusion.5
  20.1 11.5 %all-gather = f32[4,12,128]{2,1,0:T(8,128)S(1)} all-gather(f32[1,12,128]{2,1,0:T(8,128)S(1)} %convolution_bitcast_fusion.5), channel_id=1, replica_groups=mesh['row'=4,'col'=8] {'row'}, dimensions={0}, use_global_device_ids=true | all-gather | bytes 30720 | tf_op jit(solution)/shard_map/all_gather | solution.py:57
  31.9 21.2 %psum.56 = f32[96,128]{1,0:T(8,128)S(1)} all-reduce(f32[96,128]{1,0:T(8,128)S(1)} %convolution_bitcast_fusion.3), channel_id=1, replica_groups=mesh['row'=4,'col'=8] {'col'}, use_global_device_ids=true, to_apply=%region_1.2 | all-reduce | flops 12288 | bytes 98304 | tf_op jit(solution)/shard_map/psum | solution.py:59
  53.1 16.4 %psum.57 = f32[96,128]{1,0:T(8,128)S(1)} all-reduce(f32[96,128]{1,0:T(8,128)S(1)} %broadcast_select_fusion.1), channel_id=1, replica_groups=mesh['row'=4,'col'=8] {'row'}, use_global_device_ids=true, to_apply=%region_2.3 | all-reduce | flops 12288 | bytes 98304 | tf_op jit(solution)/shard_map/psum | solution.py:17
  69.5 1.7 fusion.39
  71.2 0.9 multiply_reduce_fusion.1
  72.1 0.9 fusion.40
  73.0 44.6 %all-reduce.1 = (f32[128]{0:T(128)S(1)}, f32[128]{0:T(128)S(1)}) all-reduce(f32[128]{0:T(128)S(1)} %get-tuple-element.17, f32[128]{0:T(128)S(1)} %fusion.40), channel_id=1, replica_groups=mesh['row'=4,'col'=8] {'row','col'}, use_global_device_ids=true, to_apply=%region_4.5 | all-reduce | flops 256 | bytes 2048 | tf_op jit(solution)/shard_map/psum | solution.py:71
  117.7 2.4 %fusion.20 = f32[1024,128]{0,1:T(8,128)S(1)} fusion(bf16[1,1,1024,1024]{3,2,1,0:T(8,128)(2,1)} %param.9, bf16[1,1,1024,128]{2,3,1,0:T(8,128)(2,1)S(1)} %copy.15, f32[1024,128]{0,1:T(8,128)S(1)} %get-tuple-element.18, f32[128]{0:T(128)S(1)} %div.18, f32[1024]{0:T(1024)S(1)} %neg.10, f32[1024]{0:T(1024)S(1)} %select_reduce_fusion), kind=kOutput, calls=%fused_computation.18 | convolution fusion | flops 269484032 | bytes 3416576 | tf_op jit(solution)/shard_map/dot_general | solution.py:47
  120.2 1.9 collective-permute-start.4
  122.1 1.9 collective-permute-start.7
  124.0 3.9 %collective-permute-start.6 = (f32[256,128]{0,1:T(8,128)S(1)}, f32[256,128]{0,1:T(8,128)S(1)}, u32[]{:S(2)}, u32[]{:S(2)}) collective-permute-start(f32[256,128]{0,1:T(8,128)S(1)} %get-tuple-element.11), channel_id=1, source_target_pairs={{0,8},{8,16},{16,24},{1,9},{9,17},{17,25},{2,10},{10,18},{18,26},{... | collective-permute-start | bytes 393224 | tf_op jit(solution)/shard_map/ppermute | solution.py:12
  128.0 3.1 %collective-permute-start.5 = (f32[256,128]{0,1:T(8,128)S(1)}, f32[256,128]{0,1:T(8,128)S(1)}, u32[]{:S(2)}, u32[]{:S(2)}) collective-permute-start(f32[256,128]{0,1:T(8,128)S(1)} %get-tuple-element.12), channel_id=1, source_target_pairs={{1,0},{2,1},{3,2},{4,3},{5,4},{6,5},{7,6},{9,8},{10,9},{11,10},{12... | collective-permute-start | bytes 393224 | tf_op jit(solution)/shard_map/ppermute | solution.py:12
  131.1 2.4 %collective-permute-done.5 = f32[256,128]{0,1:T(8,128)S(1)} collective-permute-done((f32[256,128]{0,1:T(8,128)S(1)}, f32[256,128]{0,1:T(8,128)S(1)}, u32[]{:S(2)}, u32[]{:S(2)}) %collective-permute-start.5) | collective-permute-done | bytes 131104 | tf_op jit(solution)/shard_map/ppermute | solution.py:12
  134.2 11.3 %all-gather.1 = f32[4,12,128]{2,1,0:T(8,128)S(1)} all-gather(f32[1,12,128]{2,1,0:T(8,128)S(1)} %convolution_bitcast_fusion.4), channel_id=1, replica_groups=mesh['row'=4,'col'=8] {'row'}, dimensions={0}, use_global_device_ids=true | all-gather | bytes 30720 | tf_op jit(solution)/shard_map/all_gather | solution.py:57
  146.1 1.0 convolution_bitcast_fusion.2
  147.2 20.5 %psum.60 = f32[96,128]{1,0:T(8,128)S(1)} all-reduce(f32[96,128]{1,0:T(8,128)S(1)} %convolution_bitcast_fusion.2), channel_id=1, replica_groups=mesh['row'=4,'col'=8] {'col'}, use_global_device_ids=true, to_apply=%region_7.8 | all-reduce | flops 12288 | bytes 98304 | tf_op jit(solution)/shard_map/psum | solution.py:59
  167.7 16.3 %psum.61 = f32[96,128]{1,0:T(8,128)S(1)} all-reduce(f32[96,128]{1,0:T(8,128)S(1)} %broadcast_select_fusion), channel_id=1, replica_groups=mesh['row'=4,'col'=8] {'row'}, use_global_device_ids=true, to_apply=%region_8.9 | all-reduce | flops 12288 | bytes 98304 | tf_op jit(solution)/shard_map/psum | solution.py:17
  184.0 1.9 fusion.38
  185.9 0.9 multiply_reduce_fusion
  186.9 0.9 fusion.43
  187.8 44.8 %all-reduce = (f32[128]{0:T(128)S(1)}, f32[128]{0:T(128)S(1)}) all-reduce(f32[128]{0:T(128)S(1)} %get-tuple-element.19, f32[128]{0:T(128)S(1)} %fusion.43), channel_id=1, replica_groups=mesh['row'=4,'col'=8] {'row','col'}, use_global_device_ids=true, to_apply=%region_10.11 | all-reduce | flops 256 | bytes 2048 | tf_op jit(solution)/shard_map/psum | solution.py:71
  232.6 1.0 fusion.57
  233.6 1.8 copy.16
  (53 shorter events, 2.8 us)
Async XLA Ops:
  0.0 71.2 %copy-start = (bf16[1,1,1024,1024]{3,2,1,0:T(8,128)(2,1)S(1)}, bf16[1,1,1024,1024]{3,2,1,0:T(8,128)(2,1)}, u32[]{:S(2)}) copy-start(bf16[1,1,1024,1024]{3,2,1,0:T(8,128)(2,1)} %param.10) | copy-start | bytes 6291460
  0.9 116.7 %copy-start.8 = (f32[1024]{0:T(1024)}, f32[1024]{0:T(1024)S(1)}, u32[]{:S(2)}) copy-start(f32[1024]{0:T(1024)S(1)} %select_reduce_fusion) | copy-start | bytes 12292
  1.0 116.7 %copy-start.11 = (f32[1024]{0:T(1024)}, f32[1024]{0:T(1024)S(1)}, u32[]{:S(2)}) copy-start(f32[1024]{0:T(1024)S(1)} %neg.10) | copy-start | bytes 12292
  2.1 14.1 %copy-start.16 = (s32[1,1,4]{2,1,0:T(1,128)S(1)}, s32[1,1,4]{2,1,0:T(1,128)}, u32[]{:S(2)}) copy-start(s32[1,1,4]{2,1,0:T(1,128)} %param.15) | copy-start | bytes 52
  2.1 16.6 %copy-start.3 = (f32[1,1,12,1024]{3,1,2,0:T(1,128)S(1)}, f32[1,1,12,1024]{3,1,2,0:T(1,128)}, u32[]{:S(2)}) copy-start(f32[1,1,12,1024]{3,1,2,0:T(1,128)} %param.11) | copy-start | bytes 147460
  2.1 29.5 %copy-start.10 = (f32[96,48]{0,1:T(8,128)S(1)}, f32[96,48]{0,1:T(8,128)}, u32[]{:S(2)}) copy-start(f32[96,48]{0,1:T(8,128)} %param.12) | copy-start | bytes 55300
  5.3 11.0 %collective-permute-start = (f32[256,128]{0,1:T(8,128)}, f32[256,128]{0,1:T(8,128)S(1)}, u32[]{:S(2)}, u32[]{:S(2)}) collective-permute-start(f32[256,128]{0,1:T(8,128)} %get-tuple-element.13), channel_id=1, source_target_pairs={{0,1},{1,2},{2,3},{3,4},{4,5},{5,6},{6,7},{8,9},{9,10},{10,11},{11... | collective-permute-start | bytes 393224 | tf_op jit(solution)/shard_map/ppermute | solution.py:12
  7.2 9.1 %collective-permute-start.3 = (f32[256,128]{0,1:T(8,128)}, f32[256,128]{0,1:T(8,128)S(1)}, u32[]{:S(2)}, u32[]{:S(2)}) collective-permute-start(f32[256,128]{0,1:T(8,128)} %get-tuple-element.14), channel_id=1, source_target_pairs={{8,0},{16,8},{24,16},{9,1},{17,9},{25,17},{10,2},{18,10},{26,18},{... | collective-permute-start | bytes 393224 | tf_op jit(solution)/shard_map/ppermute | solution.py:12
  9.6 7.1 %collective-permute-start.2 = (f32[256,128]{0,1:T(8,128)}, f32[256,128]{0,1:T(8,128)S(1)}, u32[]{:S(2)}, u32[]{:S(2)}) collective-permute-start(f32[256,128]{0,1:T(8,128)} %get-tuple-element.15), channel_id=1, source_target_pairs={{0,8},{8,16},{16,24},{1,9},{9,17},{17,25},{2,10},{10,18},{18,26},{... | collective-permute-start | bytes 393224 | tf_op jit(solution)/shard_map/ppermute | solution.py:12
  13.1 5.6 %collective-permute-start.1 = (f32[256,128]{0,1:T(8,128)S(1)}, f32[256,128]{0,1:T(8,128)}, u32[]{:S(2)}, u32[]{:S(2)}) collective-permute-start(f32[256,128]{0,1:T(8,128)S(1)} %get-tuple-element.16), channel_id=1, source_target_pairs={{1,0},{2,1},{3,2},{4,3},{5,4},{6,5},{7,6},{9,8},{10,9},{11,10},{12... | collective-permute-start | bytes 393224 | tf_op jit(solution)/shard_map/ppermute | solution.py:12
  16.3 117.3 %copy-start.13 = (f32[1,2,4,128]{3,1,2,0:T(2,128)}, f32[1,2,4,128]{3,1,2,0:T(2,128)S(1)}, u32[]{:S(2)}) copy-start(f32[1,2,4,128]{3,1,2,0:T(2,128)S(1)} %copy.18) | copy-start | bytes 12292
  69.5 2.6 %copy-start.1 = (bf16[1,1,1024,1024]{3,2,1,0:T(8,128)(2,1)S(1)}, bf16[1,1,1024,1024]{3,2,1,0:T(8,128)(2,1)}, u32[]{:S(2)}) copy-start(bf16[1,1,1024,1024]{3,2,1,0:T(8,128)(2,1)} %param.9) | copy-start | bytes 6291460
  117.7 2.5 %copy-start.14 = (f32[128]{0:T(128)}, f32[128]{0:T(128)S(1)}, u32[]{:S(2)}) copy-start(f32[128]{0:T(128)S(1)} %div.18) | copy-start | bytes 1540
  120.2 10.9 %collective-permute-start.4 = (f32[256,128]{0,1:T(8,128)S(1)}, f32[256,128]{0,1:T(8,128)S(1)}, u32[]{:S(2)}, u32[]{:S(2)}) collective-permute-start(f32[256,128]{0,1:T(8,128)S(1)} %get-tuple-element.9), channel_id=1, source_target_pairs={{0,1},{1,2},{2,3},{3,4},{4,5},{5,6},{6,7},{8,9},{9,10},{10,11},{11... | collective-permute-start | bytes 393224 | tf_op jit(solution)/shard_map/ppermute | solution.py:12
  122.1 9.0 %collective-permute-start.7 = (f32[256,128]{0,1:T(8,128)S(1)}, f32[256,128]{0,1:T(8,128)S(1)}, u32[]{:S(2)}, u32[]{:S(2)}) collective-permute-start(f32[256,128]{0,1:T(8,128)S(1)} %get-tuple-element.10), channel_id=1, source_target_pairs={{8,0},{16,8},{24,16},{9,1},{17,9},{25,17},{10,2},{18,10},{26,18},{... | collective-permute-start | bytes 393224 | tf_op jit(solution)/shard_map/ppermute | solution.py:12
  124.0 7.1 %collective-permute-start.6 = (f32[256,128]{0,1:T(8,128)S(1)}, f32[256,128]{0,1:T(8,128)S(1)}, u32[]{:S(2)}, u32[]{:S(2)}) collective-permute-start(f32[256,128]{0,1:T(8,128)S(1)} %get-tuple-element.11), channel_id=1, source_target_pairs={{0,8},{8,16},{16,24},{1,9},{9,17},{17,25},{2,10},{10,18},{18,26},{... | collective-permute-start | bytes 393224 | tf_op jit(solution)/shard_map/ppermute | solution.py:12
  128.0 5.6 %collective-permute-start.5 = (f32[256,128]{0,1:T(8,128)S(1)}, f32[256,128]{0,1:T(8,128)S(1)}, u32[]{:S(2)}, u32[]{:S(2)}) collective-permute-start(f32[256,128]{0,1:T(8,128)S(1)} %get-tuple-element.12), channel_id=1, source_target_pairs={{1,0},{2,1},{3,2},{4,3},{5,4},{6,5},{7,6},{9,8},{10,9},{11,10},{12... | collective-permute-start | bytes 393224 | tf_op jit(solution)/shard_map/ppermute | solution.py:12
  131.1 2.5 %copy-start.4 = (f32[256,128]{0,1:T(8,128)}, f32[256,128]{0,1:T(8,128)S(1)}, u32[]{:S(2)}) copy-start(f32[256,128]{0,1:T(8,128)S(1)} %collective-permute-done.4) | copy-start | bytes 393220
  131.1 3.0 %copy-start.5 = (f32[256,128]{0,1:T(8,128)}, f32[256,128]{0,1:T(8,128)S(1)}, u32[]{:S(2)}) copy-start(f32[256,128]{0,1:T(8,128)S(1)} %collective-permute-done.7) | copy-start | bytes 393220
  131.1 3.0 %copy-start.6 = (f32[256,128]{0,1:T(8,128)}, f32[256,128]{0,1:T(8,128)S(1)}, u32[]{:S(2)}) copy-start(f32[256,128]{0,1:T(8,128)S(1)} %collective-permute-done.6) | copy-start | bytes 393220
  133.6 0.7 copy-start.7
  184.0 2.9 %copy-start.2 = (bf16[1,1,1024,1024]{3,2,1,0:T(8,128)(2,1)S(1)}, bf16[1,1,1024,1024]{3,2,1,0:T(8,128)(2,1)}, u32[]{:S(2)}) copy-start(bf16[1,1,1024,1024]{3,2,1,0:T(8,128)(2,1)} %param.9) | copy-start | bytes 6291460
  185.9 46.7 %copy-start.9 = (f32[1024]{0:T(1024)S(1)}, f32[1024]{0:T(1024)}, u32[]{:S(2)}) copy-start(f32[1024]{0:T(1024)} %copy-done.8) | copy-start | bytes 12292
  185.9 46.7 %copy-start.12 = (f32[1024]{0:T(1024)S(1)}, f32[1024]{0:T(1024)}, u32[]{:S(2)}) copy-start(f32[1024]{0:T(1024)} %copy-done.11) | copy-start | bytes 12292
  185.9 46.6 %copy-start.15 = (f32[128]{0:T(128)S(1)}, f32[128]{0:T(128)}, u32[]{:S(2)}) copy-start(f32[128]{0:T(128)} %copy-done.14) | copy-start | bytes 1540
where the time goes:
time: 236 us; the launch traced here: 235 us
  blocking collectives  187 us (79%)
  starting transfers between devices  21.7 us (9%)
  matrix products  15.4 us (7%)
  waiting for transfers between devices  4.82 us (2%)
  local copies, waits for them, and re-layouts  4.43 us (2%)
    psum x2, blocking collectives, local(): gain = lax.psum(gain_local, ('row', 'col'))  89.4 us
    psum x2, blocking collectives, local(): total = lax.psum(partial_value, 'col')  41.7 us
    psum x2, blocking collectives, broadcast(): return lax.psum(block, axis)  32.7 us
    all_gather x2, blocking collectives, local(): gathered = lax.all_gather(corner_force, 'row', axis=0, tiled=True)  22.8 us
    ppermute x8, starting transfers between devices, passed_along(): return lax.ppermute(x, axis, pairs)  21.7 us
    dot_general x2, matrix products, local(): jnp.dot(flex_block, lam.astype(jnp.bfloat16), preferred_element_type=jnp....  4.86 us
    ppermute x8, waiting for transfers between devices, passed_along(): return lax.ppermute(x, axis, pairs)  4.82 us
  transfers between devices with their start and end apart: 8, of which 3 were waited for; matrix products, arithmetic and copies ran while one was open for 0% of the time, Pallas kernels for 0%

commit v1 on v0

--- a/solution.py
+++ b/solution.py
@@ -56,7 +56,7 @@
         corner_force = jnp.dot(coupling, jump, precision=lax.Precision.HIGHEST)
         gathered = lax.all_gather(corner_force, "row", axis=0, tiled=True)
         partial_value = jnp.dot(coarse_inverse, gathered, precision=lax.Precision.HIGHEST)
-        total = lax.psum(partial_value, "col")
+        total = jnp.sum(lax.all_gather(partial_value, "col"), axis=0)
         picked = broadcast(total, "row", col_index // 2)
         offset = col_index % 2 * (corners * row_devices) + row_index * corners
         coarse = lax.dynamic_slice_in_dim(picked, offset, corners, 0)

time: 236 us -> 211 us (0.89)
  blocking collectives: 187 us -> 161 us
    psum x2 -> x0, blocking collectives: 41.7 us -> none  [local(): total = lax.psum(partial_value, 'col')]
    all_gather x0 -> x2, blocking collectives: none -> 20.9 us  [local(): total = jnp.sum(lax.all_gather(partial_value, 'col'), axis=0)]
    psum x2, blocking collectives: 89.4 us -> 84.3 us  [local(): gain = lax.psum(gain_local, ('row', 'col'))]
where the time goes in v1:
time: 211 us; the launch traced here: 210 us
  blocking collectives  161 us (76%)
  starting transfers between devices  21.7 us (10%)
  matrix products  14.6 us (7%)
  waiting for transfers between devices  5.12 us (2%)
  local copies, waits for them, and re-layouts  3.87 us (2%)
  other arithmetic  3.06 us (1%)
    psum x2, blocking collectives, local(): gain = lax.psum(gain_local, ('row', 'col'))  84.3 us
    psum x2, blocking collectives, broadcast(): return lax.psum(block, axis)  32.8 us
    all_gather x2, blocking collectives, local(): gathered = lax.all_gather(corner_force, 'row', axis=0, tiled=True)  22.8 us
    ppermute x8, starting transfers between devices, passed_along(): return lax.ppermute(x, axis, pairs)  21.7 us
    all_gather x2, blocking collectives, local(): total = jnp.sum(lax.all_gather(partial_value, 'col'), axis=0)  20.9 us
    ppermute x8, waiting for transfers between devices, passed_along(): return lax.ppermute(x, axis, pairs)  5.12 us
    dot_general x2, matrix products, local(): jnp.dot(flex_block, lam.astype(jnp.bfloat16), preferred_element_type=jnp....  4.85 us
  transfers between devices with their start and end apart: 8, of which 3 were waited for; matrix products, arithmetic and copies ran while one was open for 0% of the time, Pallas kernels for 0%

profile of v1, /device:TPU:14, one launch (start us, length us, event | category | flops | bytes accessed | tf_op | source)
XLA Modules:
  0.0 209.5 jit_solution(5367946401894328059)
XLA Ops:
  0.0 0.9 select_reduce_fusion
  1.0 1.1 copy.15
  2.1 2.4 %fusion.14 = f32[1024,128]{0,1:T(8,128)S(1)} fusion(bf16[1,1,1024,1024]{3,2,1,0:T(8,128)(2,1)} %param.9, bf16[1,1,1024,128]{2,3,1,0:T(8,128)(2,1)S(1)} %copy.15, f32[1024]{0:T(1024)S(1)} %neg.10, f32[1024]{0:T(1024)S(1)} %select_reduce_fusion), kind=kOutput, calls=%fused_computation.16 | convolution fusion | flops 269221888 | bytes 2891776 | tf_op jit(solution)/shard_map/dot_general | solution.py:47
  5.3 1.9 collective-permute-start
  7.2 2.4 %collective-permute-start.3 = (f32[256,128]{0,1:T(8,128)}, f32[256,128]{0,1:T(8,128)S(1)}, u32[]{:S(2)}, u32[]{:S(2)}) collective-permute-start(f32[256,128]{0,1:T(8,128)} %get-tuple-element.14), channel_id=1, source_target_pairs={{8,0},{16,8},{24,16},{9,1},{17,9},{25,17},{10,2},{18,10},{26,18},{... | collective-permute-start | bytes 393224 | tf_op jit(solution)/shard_map/ppermute | solution.py:12
  9.6 3.5 %collective-permute-start.2 = (f32[256,128]{0,1:T(8,128)}, f32[256,128]{0,1:T(8,128)S(1)}, u32[]{:S(2)}, u32[]{:S(2)}) collective-permute-start(f32[256,128]{0,1:T(8,128)} %get-tuple-element.15), channel_id=1, source_target_pairs={{0,8},{8,16},{16,24},{1,9},{9,17},{17,25},{2,10},{10,18},{18,26},{... | collective-permute-start | bytes 393224 | tf_op jit(solution)/shard_map/ppermute | solution.py:12
  13.1 3.1 %collective-permute-start.1 = (f32[256,128]{0,1:T(8,128)}, f32[256,128]{0,1:T(8,128)S(1)}, u32[]{:S(2)}, u32[]{:S(2)}) collective-permute-start(f32[256,128]{0,1:T(8,128)} %get-tuple-element.16), channel_id=1, source_target_pairs={{1,0},{2,1},{3,2},{4,3},{5,4},{6,5},{7,6},{9,8},{10,9},{11,10},{12... | collective-permute-start | bytes 393224 | tf_op jit(solution)/shard_map/ppermute | solution.py:12
  16.7 2.3 %collective-permute-done.1 = f32[256,128]{0,1:T(8,128)S(1)} collective-permute-done((f32[256,128]{0,1:T(8,128)}, f32[256,128]{0,1:T(8,128)S(1)}, u32[]{:S(2)}, u32[]{:S(2)}) %collective-permute-start.1) | collective-permute-done | bytes 131104 | tf_op jit(solution)/shard_map/ppermute | solution.py:12
  19.5 11.4 %all-gather.2 = f32[4,12,128]{2,1,0:T(8,128)S(1)} all-gather(f32[1,12,128]{2,1,0:T(8,128)S(1)} %convolution_bitcast_fusion.5), channel_id=1, replica_groups=mesh['row'=4,'col'=8] {'row'}, dimensions={0}, use_global_device_ids=true | all-gather | bytes 30720 | tf_op jit(solution)/shard_map/all_gather | solution.py:57
  31.0 1.0 convolution_bitcast_fusion.3
  32.0 9.5 %all-gather = f32[768,128]{1,0:T(8,128)S(1)} all-gather(f32[96,128]{1,0:T(8,128)S(1)} %convolution_bitcast_fusion.3), channel_id=2, replica_groups=mesh['row'=4,'col'=8] {'col'}, dimensions={0}, use_global_device_ids=true | all-gather | bytes 442368 | tf_op jit(solution)/shard_map/all_gather | solution.py:59
  41.6 16.5 %psum.42 = f32[96,128]{1,0:T(8,128)S(1)} all-reduce(f32[96,128]{1,0:T(8,128)S(1)} %broadcast_select_fusion.1), channel_id=1, replica_groups=mesh['row'=4,'col'=8] {'row'}, use_global_device_ids=true, to_apply=%region_2.3 | all-reduce | flops 12288 | bytes 98304 | tf_op jit(solution)/shard_map/psum | solution.py:17
  58.1 1.8 fusion.39
  60.0 0.9 multiply_reduce_fusion.1
  60.9 0.9 fusion.40
  61.8 42.0 %all-reduce.1 = (f32[128]{0:T(128)S(1)}, f32[128]{0:T(128)S(1)}) all-reduce(f32[128]{0:T(128)S(1)} %get-tuple-element.17, f32[128]{0:T(128)S(1)} %fusion.40), channel_id=1, replica_groups=mesh['row'=4,'col'=8] {'row','col'}, use_global_device_ids=true, to_apply=%region_4.5 | all-reduce | flops 256 | bytes 2048 | tf_op jit(solution)/shard_map/psum | solution.py:71
  103.9 2.4 %fusion.20 = f32[1024,128]{0,1:T(8,128)S(1)} fusion(bf16[1,1,1024,1024]{3,2,1,0:T(8,128)(2,1)} %param.9, bf16[1,1,1024,128]{2,3,1,0:T(8,128)(2,1)S(1)} %copy.15, f32[1024,128]{0,1:T(8,128)S(1)} %get-tuple-element.18, f32[128]{0:T(128)S(1)} %div.18, f32[1024]{0:T(1024)S(1)} %neg.10, f32[1024]{0:T(1024)S(1)} %select_reduce_fusion), kind=kOutput, calls=%fused_computation.18 | convolution fusion | flops 269484032 | bytes 3416576 | tf_op jit(solution)/shard_map/dot_general | solution.py:47
  106.4 1.9 collective-permute-start.4
  108.3 1.9 collective-permute-start.7
  110.2 3.9 %collective-permute-start.6 = (f32[256,128]{0,1:T(8,128)S(1)}, f32[256,128]{0,1:T(8,128)S(1)}, u32[]{:S(2)}, u32[]{:S(2)}) collective-permute-start(f32[256,128]{0,1:T(8,128)S(1)} %get-tuple-element.11), channel_id=1, source_target_pairs={{0,8},{8,16},{16,24},{1,9},{9,17},{17,25},{2,10},{10,18},{18,26},{... | collective-permute-start | bytes 393224 | tf_op jit(solution)/shard_map/ppermute | solution.py:12
  114.2 3.1 %collective-permute-start.5 = (f32[256,128]{0,1:T(8,128)S(1)}, f32[256,128]{0,1:T(8,128)S(1)}, u32[]{:S(2)}, u32[]{:S(2)}) collective-permute-start(f32[256,128]{0,1:T(8,128)S(1)} %get-tuple-element.12), channel_id=1, source_target_pairs={{1,0},{2,1},{3,2},{4,3},{5,4},{6,5},{7,6},{9,8},{10,9},{11,10},{12... | collective-permute-start | bytes 393224 | tf_op jit(solution)/shard_map/ppermute | solution.py:12
  117.3 2.4 %collective-permute-done.5 = f32[256,128]{0,1:T(8,128)S(1)} collective-permute-done((f32[256,128]{0,1:T(8,128)S(1)}, f32[256,128]{0,1:T(8,128)S(1)}, u32[]{:S(2)}, u32[]{:S(2)}) %collective-permute-start.5) | collective-permute-done | bytes 131104 | tf_op jit(solution)/shard_map/ppermute | solution.py:12
  120.4 11.3 %all-gather.3 = f32[4,12,128]{2,1,0:T(8,128)S(1)} all-gather(f32[1,12,128]{2,1,0:T(8,128)S(1)} %convolution_bitcast_fusion.4), channel_id=1, replica_groups=mesh['row'=4,'col'=8] {'row'}, dimensions={0}, use_global_device_ids=true | all-gather | bytes 30720 | tf_op jit(solution)/shard_map/all_gather | solution.py:57
  132.0 11.4 %all-gather.1 = f32[768,128]{1,0:T(8,128)} all-gather(f32[96,128]{1,0:T(8,128)S(1)} %convolution_bitcast_fusion.2), channel_id=3, replica_groups=mesh['row'=4,'col'=8] {'col'}, dimensions={0}, use_global_device_ids=true | all-gather | bytes 442368 | tf_op jit(solution)/shard_map/all_gather | solution.py:59
  143.4 1.0 reduce_sum.67
  144.5 16.3 %psum.45 = f32[96,128]{1,0:T(8,128)S(1)} all-reduce(f32[96,128]{1,0:T(8,128)S(1)} %broadcast_select_fusion), channel_id=1, replica_groups=mesh['row'=4,'col'=8] {'row'}, use_global_device_ids=true, to_apply=%region_8.9 | all-reduce | flops 12288 | bytes 98304 | tf_op jit(solution)/shard_map/psum | solution.py:17
  160.8 1.9 fusion.38
  162.7 0.9 multiply_reduce_fusion
  163.6 0.9 fusion.43
  164.5 42.2 %all-reduce = (f32[128]{0:T(128)S(1)}, f32[128]{0:T(128)S(1)}) all-reduce(f32[128]{0:T(128)S(1)} %get-tuple-element.19, f32[128]{0:T(128)S(1)} %fusion.43), channel_id=1, replica_groups=mesh['row'=4,'col'=8] {'row','col'}, use_global_device_ids=true, to_apply=%region_10.11 | all-reduce | flops 256 | bytes 2048 | tf_op jit(solution)/shard_map/psum | solution.py:71
  206.8 1.0 fusion.57
  207.7 1.8 copy.16
  (61 shorter events, 2.9 us)
Async XLA Ops:
  0.0 60.0 %copy-start = (bf16[1,1,1024,1024]{3,2,1,0:T(8,128)(2,1)S(1)}, bf16[1,1,1024,1024]{3,2,1,0:T(8,128)(2,1)}, u32[]{:S(2)}) copy-start(bf16[1,1,1024,1024]{3,2,1,0:T(8,128)(2,1)} %param.10) | copy-start | bytes 6291460
  0.9 102.9 %copy-start.11 = (f32[1024]{0:T(1024)}, f32[1024]{0:T(1024)S(1)}, u32[]{:S(2)}) copy-start(f32[1024]{0:T(1024)S(1)} %select_reduce_fusion) | copy-start | bytes 12292
  1.0 102.9 %copy-start.14 = (f32[1024]{0:T(1024)}, f32[1024]{0:T(1024)S(1)}, u32[]{:S(2)}) copy-start(f32[1024]{0:T(1024)S(1)} %neg.10) | copy-start | bytes 12292
  2.1 14.1 %copy-start.19 = (s32[1,1,4]{2,1,0:T(1,128)S(1)}, s32[1,1,4]{2,1,0:T(1,128)}, u32[]{:S(2)}) copy-start(s32[1,1,4]{2,1,0:T(1,128)} %param.15) | copy-start | bytes 52
  2.1 16.9 %copy-start.3 = (f32[1,1,12,1024]{3,1,2,0:T(1,128)S(1)}, f32[1,1,12,1024]{3,1,2,0:T(1,128)}, u32[]{:S(2)}) copy-start(f32[1,1,12,1024]{3,1,2,0:T(1,128)} %param.11) | copy-start | bytes 147460
  5.3 11.0 %collective-permute-start = (f32[256,128]{0,1:T(8,128)}, f32[256,128]{0,1:T(8,128)S(1)}, u32[]{:S(2)}, u32[]{:S(2)}) collective-permute-start(f32[256,128]{0,1:T(8,128)} %get-tuple-element.13), channel_id=1, source_target_pairs={{0,1},{1,2},{2,3},{3,4},{4,5},{5,6},{6,7},{8,9},{9,10},{10,11},{11... | collective-permute-start | bytes 393224 | tf_op jit(solution)/shard_map/ppermute | solution.py:12
  7.2 9.1 %collective-permute-start.3 = (f32[256,128]{0,1:T(8,128)}, f32[256,128]{0,1:T(8,128)S(1)}, u32[]{:S(2)}, u32[]{:S(2)}) collective-permute-start(f32[256,128]{0,1:T(8,128)} %get-tuple-element.14), channel_id=1, source_target_pairs={{8,0},{16,8},{24,16},{9,1},{17,9},{25,17},{10,2},{18,10},{26,18},{... | collective-permute-start | bytes 393224 | tf_op jit(solution)/shard_map/ppermute | solution.py:12
  9.6 7.1 %collective-permute-start.2 = (f32[256,128]{0,1:T(8,128)}, f32[256,128]{0,1:T(8,128)S(1)}, u32[]{:S(2)}, u32[]{:S(2)}) collective-permute-start(f32[256,128]{0,1:T(8,128)} %get-tuple-element.15), channel_id=1, source_target_pairs={{0,8},{8,16},{16,24},{1,9},{9,17},{17,25},{2,10},{10,18},{18,26},{... | collective-permute-start | bytes 393224 | tf_op jit(solution)/shard_map/ppermute | solution.py:12
  13.1 5.9 %collective-permute-start.1 = (f32[256,128]{0,1:T(8,128)}, f32[256,128]{0,1:T(8,128)S(1)}, u32[]{:S(2)}, u32[]{:S(2)}) collective-permute-start(f32[256,128]{0,1:T(8,128)} %get-tuple-element.16), channel_id=1, source_target_pairs={{1,0},{2,1},{3,2},{4,3},{5,4},{6,5},{7,6},{9,8},{10,9},{11,10},{12... | collective-permute-start | bytes 393224 | tf_op jit(solution)/shard_map/ppermute | solution.py:12
  16.3 103.5 %copy-start.16 = (f32[1,2,4,128]{3,1,2,0:T(2,128)}, f32[1,2,4,128]{3,1,2,0:T(2,128)S(1)}, u32[]{:S(2)}) copy-start(f32[1,2,4,128]{3,1,2,0:T(2,128)S(1)} %copy.18) | copy-start | bytes 12292
  16.3 14.7 %copy-start.4 = (f32[256,128]{0,1:T(8,128)}, f32[256,128]{0,1:T(8,128)S(1)}, u32[]{:S(2)}) copy-start(f32[256,128]{0,1:T(8,128)S(1)} %collective-permute-done.3) | copy-start | bytes 393220
  16.7 14.3 %copy-start.5 = (f32[256,128]{0,1:T(8,128)}, f32[256,128]{0,1:T(8,128)S(1)}, u32[]{:S(2)}) copy-start(f32[256,128]{0,1:T(8,128)S(1)} %collective-permute-done.2) | copy-start | bytes 393220
  19.0 12.0 %copy-start.6 = (f32[256,128]{0,1:T(8,128)}, f32[256,128]{0,1:T(8,128)S(1)}, u32[]{:S(2)}) copy-start(f32[256,128]{0,1:T(8,128)S(1)} %collective-permute-done.1) | copy-start | bytes 393220
  58.1 2.8 %copy-start.1 = (bf16[1,1,1024,1024]{3,2,1,0:T(8,128)(2,1)S(1)}, bf16[1,1,1024,1024]{3,2,1,0:T(8,128)(2,1)}, u32[]{:S(2)}) copy-start(bf16[1,1,1024,1024]{3,2,1,0:T(8,128)(2,1)} %param.9) | copy-start | bytes 6291460
  103.9 2.5 %copy-start.17 = (f32[128]{0:T(128)}, f32[128]{0:T(128)S(1)}, u32[]{:S(2)}) copy-start(f32[128]{0:T(128)S(1)} %div.18) | copy-start | bytes 1540
  106.3 25.4 %copy-start.13 = (f32[96,48]{0,1:T(8,128)S(1)}, f32[96,48]{0,1:T(8,128)}, u32[]{:S(2)}) copy-start(f32[96,48]{0,1:T(8,128)} %param.12) | copy-start | bytes 55300
  106.4 10.9 %collective-permute-start.4 = (f32[256,128]{0,1:T(8,128)S(1)}, f32[256,128]{0,1:T(8,128)S(1)}, u32[]{:S(2)}, u32[]{:S(2)}) collective-permute-start(f32[256,128]{0,1:T(8,128)S(1)} %get-tuple-element.9), channel_id=1, source_target_pairs={{0,1},{1,2},{2,3},{3,4},{4,5},{5,6},{6,7},{8,9},{9,10},{10,11},{11... | collective-permute-start | bytes 393224 | tf_op jit(solution)/shard_map/ppermute | solution.py:12
  108.3 9.0 %collective-permute-start.7 = (f32[256,128]{0,1:T(8,128)S(1)}, f32[256,128]{0,1:T(8,128)S(1)}, u32[]{:S(2)}, u32[]{:S(2)}) collective-permute-start(f32[256,128]{0,1:T(8,128)S(1)} %get-tuple-element.10), channel_id=1, source_target_pairs={{8,0},{16,8},{24,16},{9,1},{17,9},{25,17},{10,2},{18,10},{26,18},{... | collective-permute-start | bytes 393224 | tf_op jit(solution)/shard_map/ppermute | solution.py:12
  110.2 7.1 %collective-permute-start.6 = (f32[256,128]{0,1:T(8,128)S(1)}, f32[256,128]{0,1:T(8,128)S(1)}, u32[]{:S(2)}, u32[]{:S(2)}) collective-permute-start(f32[256,128]{0,1:T(8,128)S(1)} %get-tuple-element.11), channel_id=1, source_target_pairs={{0,8},{8,16},{16,24},{1,9},{9,17},{17,25},{2,10},{10,18},{18,26},{... | collective-permute-start | bytes 393224 | tf_op jit(solution)/shard_map/ppermute | solution.py:12
  114.2 5.6 %collective-permute-start.5 = (f32[256,128]{0,1:T(8,128)S(1)}, f32[256,128]{0,1:T(8,128)S(1)}, u32[]{:S(2)}, u32[]{:S(2)}) collective-permute-start(f32[256,128]{0,1:T(8,128)S(1)} %get-tuple-element.12), channel_id=1, source_target_pairs={{1,0},{2,1},{3,2},{4,3},{5,4},{6,5},{7,6},{9,8},{10,9},{11,10},{12... | collective-permute-start | bytes 393224 | tf_op jit(solution)/shard_map/ppermute | solution.py:12
  117.3 2.5 %copy-start.7 = (f32[256,128]{0,1:T(8,128)}, f32[256,128]{0,1:T(8,128)S(1)}, u32[]{:S(2)}) copy-start(f32[256,128]{0,1:T(8,128)S(1)} %collective-permute-done.4) | copy-start | bytes 393220
  117.3 3.0 %copy-start.8 = (f32[256,128]{0,1:T(8,128)}, f32[256,128]{0,1:T(8,128)S(1)}, u32[]{:S(2)}) copy-start(f32[256,128]{0,1:T(8,128)S(1)} %collective-permute-done.7) | copy-start | bytes 393220
  117.3 3.0 %copy-start.9 = (f32[256,128]{0,1:T(8,128)}, f32[256,128]{0,1:T(8,128)S(1)}, u32[]{:S(2)}) copy-start(f32[256,128]{0,1:T(8,128)S(1)} %collective-permute-done.6) | copy-start | bytes 393220
  119.8 0.7 copy-start.10
  160.8 2.8 %copy-start.2 = (bf16[1,1,1024,1024]{3,2,1,0:T(8,128)(2,1)S(1)}, bf16[1,1,1024,1024]{3,2,1,0:T(8,128)(2,1)}, u32[]{:S(2)}) copy-start(bf16[1,1,1024,1024]{3,2,1,0:T(8,128)(2,1)} %param.9) | copy-start | bytes 6291460
  162.7 44.1 %copy-start.12 = (f32[1024]{0:T(1024)S(1)}, f32[1024]{0:T(1024)}, u32[]{:S(2)}) copy-start(f32[1024]{0:T(1024)} %copy-done.11) | copy-start | bytes 12292
  162.7 44.1 %copy-start.15 = (f32[1024]{0:T(1024)S(1)}, f32[1024]{0:T(1024)}, u32[]{:S(2)}) copy-start(f32[1024]{0:T(1024)} %copy-done.14) | copy-start | bytes 12292
  162.7 44.1 %copy-start.18 = (f32[128]{0:T(128)S(1)}, f32[128]{0:T(128)}, u32[]{:S(2)}) copy-start(f32[128]{0:T(128)} %copy-done.17) | copy-start | bytes 1540
